TPU v7x, 32 devices: a whole 2x2x4 slice. The times are simulated.
32 devices in a mesh: batch: 8 (over z, x), owner: 4 (over y, core).
Axes of the slice: x: 2, y: 2, z: 4, core: 2. Of those that a mesh axis runs over, the one named last changes fastest.
Arguments:
- queries: bfloat16 [128, 32, 128], P(('batch', 'owner')), may hold values from -8 to 8
- pool: bfloat16 [32, 184, 128], P(('owner', 'batch')), may hold values from -20 to 20
- lengths: int32 [32], P('owner'), may hold values from 46 to 180, as said below
- candidates: int32 [128, 12], P('batch'), may hold values from 0 to 31, as said below
- owner_map: int32 [32], replicated, may hold values from 0 to 31, as said below
- teacher: float32 [128, 12], P(('batch', 'owner')), may hold values from -12 to 12
Outputs:
- query_grad: float32 [128, 32, 128], P(('batch', 'owner'))
- divergence: float32 [128], P(('batch', 'owner'))
Inputs may be any that keep to these rules, and one draw needn't show every extreme that they name: `lengths`: every owner group (pool rows k * 8 to (k + 1) * 8 - 1) holds a passage of exactly 180 tokens. `owner_map`: A permutation: each pool row belongs to one passage id. Each query names 12 different passages. The owner group of a passage p is owner_map[p] // 8. All queries of one batch index have the same number of candidates in each owner group: 6 in some of the groups, 3 in half, none in a quarter; which groups these are differs between batch indices.
All inputs are finite; a program needn't handle non-finite values.
Results may differ from a plain program's by a relative error of at most 0.0075.
Values may be sent and summed in bfloat16 or wider, within the bound.
No kernel may reach another device: no remote copies, remote signals or barrier semaphores. Data moves between devices by JAX's collectives and lax.ppermute only.
A program may use at most 64 MiB of HBM per device.

v0:
```python
import math
import jax
import jax.numpy as jnp
from jax import lax
from jax.sharding import PartitionSpec as P

CPO = 3
SHARPNESS = 20.0
STUDENT_GAIN = 2.0
LOSS_SCALE = 64.0
EPSILON = 1e-06


def unit_rows(values):
    widened = values.astype(jnp.float32)
    inv_norm = lax.rsqrt(jnp.sum(widened * widened, axis=-1, keepdims=True) + EPSILON)
    return (widened * inv_norm, inv_norm)


def token_terms(query_block, passages, length_block):
    similar = jnp.einsum(
        "bid,bktd->bkit", query_block, passages, preferred_element_type=jnp.float32
    )
    in_range = lax.broadcasted_iota(jnp.int32, similar.shape, 3) < length_block[:, :, None, None]
    exp_terms = jnp.where(in_range, jnp.exp(SHARPNESS * similar), 0.0)
    return (exp_terms, jnp.sum(exp_terms, axis=3))


def loss_terms(scores, teacher_rows):
    student = STUDENT_GAIN * scores
    log_student = student - jnp.log(jnp.sum(jnp.exp(student), axis=1, keepdims=True))
    log_target = teacher_rows - jnp.log(jnp.sum(jnp.exp(teacher_rows), axis=1, keepdims=True))
    target = jnp.exp(log_target)
    divergence = jnp.sum(target * (log_target - log_student), axis=1)
    score_grad = LOSS_SCALE * STUDENT_GAIN * (jnp.exp(log_student) - target)
    return (divergence, score_grad)


def local(queries, pool, lengths, candidates, owner_map, teacher):
    own_rows = queries.shape[0]
    all_rows = candidates.shape[0]
    tok_count = queries.shape[1]
    feature = queries.shape[2]
    slot_cap = 2 * CPO
    my_group = lax.axis_index("owner")
    unit_query, inv_norm = unit_rows(queries)
    sent_query = unit_query.astype(jnp.bfloat16)
    gathered = lax.all_gather(sent_query, "owner", axis=0, tiled=True)
    shard_unit = unit_rows(pool)[0].astype(jnp.bfloat16)
    cached = lax.all_gather(shard_unit, "batch", axis=0, tiled=True)
    group_rows = cached.shape[0]
    slot_ids = jnp.take(owner_map, candidates, axis=0)
    local_slot = slot_ids - my_group * group_rows
    is_local = (local_slot >= 0) & (local_slot < group_rows)
    order_rank = jnp.cumsum(is_local.astype(jnp.int32), axis=1) - 1
    slot_iota = lax.broadcasted_iota(jnp.int32, (1, 1, slot_cap), 2)
    matches = is_local[:, :, None] & (order_rank[:, :, None] == slot_iota)
    filled = jnp.any(matches, axis=1)
    pick_slot = jnp.sum(jnp.where(matches, local_slot[:, :, None], 0), axis=1)
    length_of = jnp.where(filled, jnp.take(lengths, pick_slot, axis=0), 1)

    def block_inputs(first_row, row_span):
        query_block = lax.dynamic_slice_in_dim(gathered, first_row, row_span, 0)
        pick_block = lax.dynamic_slice_in_dim(pick_slot, first_row, row_span, 0)
        length_block = lax.dynamic_slice_in_dim(length_of, first_row, row_span, 0)
        return (query_block, jnp.take(cached, pick_block, axis=0), length_block)

    stride = math.gcd(all_rows, 8)

    def forward(block_index):
        query_block, passages, length_block = block_inputs(block_index * stride, stride)
        totals = token_terms(query_block, passages, length_block)[1]
        ratio = totals / length_block[:, :, None].astype(jnp.float32)
        return jnp.sum(jnp.log(ratio), axis=2) / SHARPNESS

    slot_scores = lax.map(forward, jnp.arange(all_rows // stride)).reshape(all_rows, slot_cap)
    dense = jnp.sum(jnp.where(matches, slot_scores[:, None, :], 0.0), axis=2)
    own_scores = lax.psum_scatter(dense, "owner", scatter_dimension=0, tiled=True)
    divergence, grad_own = loss_terms(own_scores, teacher)
    grad_rows = lax.all_gather(grad_own, "owner", axis=0, tiled=True)
    slot_grads = jnp.sum(jnp.where(matches, grad_rows[:, :, None], 0.0), axis=1)
    groups = lax.axis_size("owner")
    inner = math.gcd(all_rows, 8)

    def one_block(block_index):
        first_row = 0 + block_index * inner
        query_block, passages, length_block = block_inputs(first_row, inner)
        grad_block = lax.dynamic_slice_in_dim(slot_grads, first_row, inner, 0)
        exp_terms, totals = token_terms(query_block, passages, length_block)
        weights = (exp_terms / totals[:, :, :, None]).astype(jnp.bfloat16)
        mixed = jnp.einsum("bkit,bktd->bkid", weights, passages, preferred_element_type=jnp.float32)
        return jnp.einsum("bk,bkid->bid", grad_block, mixed, precision=lax.Precision.HIGHEST)

    partials = (
        lax.map(one_block, jnp.arange(all_rows // inner))
        .reshape(all_rows, tok_count, feature)
        .reshape(groups, own_rows, tok_count, feature)
    )
    arrived = lax.all_to_all(partials, "owner", split_axis=0, concat_axis=0, tiled=True)
    unit_grad = jnp.sum(arrived, axis=0)
    radial = jnp.sum(unit_query * unit_grad, axis=-1, keepdims=True)
    query_grad = (unit_grad - unit_query * radial) * inv_norm
    return (query_grad, divergence)


def solution(mesh):
    in_specs = (
        P(("batch", "owner"), None, None),
        P(("owner", "batch"), None, None),
        P("owner"),
        P("batch", None),
        P(),
        P(("batch", "owner"), None),
    )
    out_specs = (P(("batch", "owner"), None, None), P(("batch", "owner")))
    return jax.shard_map(local, mesh=mesh, in_specs=in_specs, out_specs=out_specs, check_vma=False)
```

profile of v0, /device:TPU:0, one launch (start us, length us, event | category | flops | bytes accessed | tf_op | source)
XLA Modules:
  0.0 102.2 jit_solution(10071462860876659092)
XLA Ops:
  0.6 0.7 compare_select_fusion.2
  1.5 1.6 %gather_fusion.2 = s32[192]{0:T(256)S(1)} fusion(s32[32]{0:T(128)S(1)} %copy-done, s32[1024]{0:T(1024)S(1)} %pad_clamp_fusion.3), kind=kCustom, calls=%fused_computation.2 | custom fusion | bytes 2304 | tf_op jit(solution)/shard_map/jit(_take)/gather | solution.py:52
  3.3 0.2 fusion.37
  4.0 1.2 %gather_fusion.3 = s32[96]{0:T(128)S(1)} fusion(s32[8]{0:T(128)S(1)} %copy-done.1, s32[1024]{0:T(1024)S(1)} %pad_clamp_fusion.2), kind=kCustom, calls=%fused_computation.3 | custom fusion | bytes 1152 | tf_op jit(solution)/shard_map/jit(_take)/gather | solution.py:60
  5.7 7.0 %all_gather.10 = bf16[16,32,128]{2,1,0:T(8,128)(2,1)} all-gather(bf16[4,32,128]{2,1,0:T(8,128)(2,1)S(1)} %fusion.32), channel_id=1, replica_groups=mesh['batch'=8,'owner'=4] {'owner'}, dimensions={0}, use_global_device_ids=true | all-gather | bytes 163840 | tf_op jit(solution)/shard_map/all_gather | solution.py:48
  12.9 31.8 %all_gather.9 = bf16[8,184,128]{2,1,0:T(8,128)(2,1)S(1)} all-gather(bf16[1,184,128]{2,1,0:T(8,128)(2,1)S(1)} %fusion.30), channel_id=1, replica_groups=mesh['batch'=8,'owner'=4] {'batch'}, dimensions={0}, use_global_device_ids=true | all-gather | bytes 423936 | tf_op jit(solution)/shard_map/all_gather | solution.py:50
  44.8 10.7 %while.20 = (s32[]{:T(128)}, f32[2,8,6]{2,1,0:T(8,128)S(1)}, s32[2]{0:T(128)S(1)}, s32[16,6]{1,0:T(8,128)S(1)}, s32[16,6]{1,0:T(8,128)S(1)}, /*index=5*/bf16[8,1...) while((s32[]{:T(128)}, f32[2,8,6]{2,1,0:T(8,128)S(1)}, ...), condition=%wide.region_8.10_spmd, body=%wide.region_5.9_spmd.sunk | while | flops 74615640 | bytes 6876823 | solution.py:76
  44.8 0.7 dynamic_slice.51
  46.2 1.0 gather_fusion
  47.3 2.5 %fusion.56 = f32[8,6,32]{2,1,0:T(8,128)S(1)} fusion(bf16[8,6,184,128]{3,2,1,0:T(8,128)(2,1)S(1)} %bitcast.65, pred[8,6]{1,0:T(8,128)(4,1)S(1)} %get-tuple-element.291, s32[8,6]{1,0:T(8,128)S(1)} %get-tuple-element.292, bf16[16,32,128]{2,1,0:T(8,128)(2,1)} %get-tuple-element.332, s32[]{:T(128)S(6)} %select_n.129), kind=kOutput, calls=%fused_computation.8.clone.1 | convolution fusion | flops 74611200 | bytes 2332916 | tf_op jit(solution)/shard_map/while/body/eval_jaxpr/bid,bktd->bkit/dot_general | solution.py:21
  50.1 0.7 dynamic_slice.51
  51.6 1.0 gather_fusion
  52.6 2.5 %fusion.56 = f32[8,6,32]{2,1,0:T(8,128)S(1)} fusion(bf16[8,6,184,128]{3,2,1,0:T(8,128)(2,1)S(1)} %bitcast.65, pred[8,6]{1,0:T(8,128)(4,1)S(1)} %get-tuple-element.291, s32[8,6]{1,0:T(8,128)S(1)} %get-tuple-element.292, bf16[16,32,128]{2,1,0:T(8,128)(2,1)} %get-tuple-element.332, s32[]{:T(128)S(6)} %select_n.129), kind=kOutput, calls=%fused_computation.8.clone.1 | convolution fusion | flops 74611200 | bytes 2332916 | tf_op jit(solution)/shard_map/while/body/eval_jaxpr/bid,bktd->bkit/dot_general | solution.py:21
  55.7 5.8 %all-reduce = f32[16,12]{1,0:T(8,128)S(1)} all-reduce(f32[16,12]{1,0:T(8,128)S(1)} %select_reduce_fusion.1), channel_id=2, replica_groups=mesh['batch'=8,'owner'=4] {'owner'}, use_global_device_ids=true, to_apply=%region_10.12.clone | all-reduce | flops 192 | bytes 1536
  61.4 0.6 dynamic-slice
  63.0 0.7 multiply_reduce_fusion
  63.7 5.2 %all-gather = f32[4,4,12]{2,1,0:T(4,128)S(1)} all-gather(f32[1,4,12]{2,1,0:T(4,128)S(1)} %get-tuple-element.199), channel_id=1, replica_groups=mesh['batch'=8,'owner'=4] {'owner'}, dimensions={0}, use_global_device_ids=true | all-gather | bytes 960 | tf_op jit(solution)/shard_map/all_gather | solution.py:80
  68.9 22.7 %while.21 = (s32[]{:T(128)}, f32[2,8,32,128]{3,2,1,0:T(8,128)}, s32[2]{0:T(128)S(1)}, f32[16,6]{0,1:T(8,128)S(1)}, s32[16,6]{1,0:T(8,128)S(1)}, /*index=5*/s32[1...) while((s32[]{:T(128)}, f32[2,8,32,128]{3,2,1,0:T(8,128)}, ...), condition=%wide.region_16.18_spmd, body=%wide.region_14.17_spmd.sunk | while | flops 150739936 | bytes 13344207 | solution.py:95
  69.0 0.7 dynamic_slice.55
  70.4 1.0 gather_fusion.1
  71.5 3.5 %bitcast_select_fusion.3 = f32[8,6,32,184]{3,2,1,0:T(8,128)} fusion(bf16[8,6,184,128]{3,2,1,0:T(8,128)(2,1)S(1)} %bitcast.66, pred[8,6]{1,0:T(8,128)(4,1)S(1)} %get-tuple-element.303, s32[8,6]{1,0:T(8,128)S(1)} %constant_dynamic-slice_fusion.4, bf16[16,32,128]{2,1,0:T(8,128)(2,1)} %get-tuple-element.368, s32[]{:T(128)S(6)} %select_n.133), kind=kOutput, calls=%fused_computation.25.clone.1 | convolution fusion | flops 74330112 | bytes 3457268 | tf_op jit(solution)/shard_map/while/body/eval_jaxpr/bid,bktd->bkit/dot_general | solution.py:21
  75.0 3.0 %fusion.61 = f32[8,6,32,128]{3,2,1,0:T(8,128)S(1)} fusion(bf16[8,6,184,128]{3,2,1,0:T(8,128)(2,1)S(1)} %bitcast.67, pred[8,6]{1,0:T(8,128)(4,1)S(1)} %get-tuple-element.303, f32[8,6,32,184]{3,2,1,0:T(8,128)} %bitcast_select_fusion.3), kind=kOutput, calls=%fused_computation.23.clone.1 | convolution fusion | flops 74049208 | bytes 4177968 | tf_op jit(solution)/shard_map/while/body/eval_jaxpr/bkit,bktd->bkid/dot_general | solution.py:91
  78.2 1.4 %fusion.62 = f32[8,1,32,128]{3,1,2,0:T(1,128)S(1)} fusion(f32[8,6,1,1]{1,2,3,0:T(1,128)S(1)} %copy.66, f32[8,6,32,128]{3,2,1,0:T(8,128)S(1)} %fusion.61), kind=kOutput, calls=%fused_computation.30.clone.1 | convolution fusion | flops 2359296 | bytes 917696 | tf_op jit(solution)/shard_map/while/body/eval_jaxpr/bk,bkid->bid/dot_general | solution.py:92
  79.6 0.7 constant_dynamic-update-slice_fusion.2
  80.3 0.7 dynamic_slice.55
  81.8 1.0 gather_fusion.1
  82.8 3.5 %bitcast_select_fusion.3 = f32[8,6,32,184]{3,2,1,0:T(8,128)} fusion(bf16[8,6,184,128]{3,2,1,0:T(8,128)(2,1)S(1)} %bitcast.66, pred[8,6]{1,0:T(8,128)(4,1)S(1)} %get-tuple-element.303, s32[8,6]{1,0:T(8,128)S(1)} %constant_dynamic-slice_fusion.4, bf16[16,32,128]{2,1,0:T(8,128)(2,1)} %get-tuple-element.368, s32[]{:T(128)S(6)} %select_n.133), kind=kOutput, calls=%fused_computation.25.clone.1 | convolution fusion | flops 74330112 | bytes 3457268 | tf_op jit(solution)/shard_map/while/body/eval_jaxpr/bid,bktd->bkit/dot_general | solution.py:21
  86.4 3.0 %fusion.61 = f32[8,6,32,128]{3,2,1,0:T(8,128)S(1)} fusion(bf16[8,6,184,128]{3,2,1,0:T(8,128)(2,1)S(1)} %bitcast.67, pred[8,6]{1,0:T(8,128)(4,1)S(1)} %get-tuple-element.303, f32[8,6,32,184]{3,2,1,0:T(8,128)} %bitcast_select_fusion.3), kind=kOutput, calls=%fused_computation.23.clone.1 | convolution fusion | flops 74049208 | bytes 4177968 | tf_op jit(solution)/shard_map/while/body/eval_jaxpr/bkit,bktd->bkid/dot_general | solution.py:91
  89.6 1.4 %fusion.62 = f32[8,1,32,128]{3,1,2,0:T(1,128)S(1)} fusion(f32[8,6,1,1]{1,2,3,0:T(1,128)S(1)} %copy.66, f32[8,6,32,128]{3,2,1,0:T(8,128)S(1)} %fusion.61), kind=kOutput, calls=%fused_computation.30.clone.1 | convolution fusion | flops 2359296 | bytes 917696 | tf_op jit(solution)/shard_map/while/body/eval_jaxpr/bk,bkid->bid/dot_general | solution.py:92
  91.0 0.7 constant_dynamic-update-slice_fusion.2
  91.7 9.4 %all_to_all.5 = f32[4,4,32,128]{3,2,1,0:T(8,128)S(1)} all-to-all(f32[4,4,32,128]{3,2,1,0:T(8,128)} %bitcast.69), channel_id=1, replica_groups=mesh['batch'=8,'owner'=4] {'owner'}, dimensions={0} | all-to-all | bytes 524288 | tf_op jit(solution)/shard_map/all_to_all | solution.py:99
  101.1 1.1 %fusion.28 = f32[4,32,128]{2,1,0:T(8,128)} fusion(f32[4,32,128]{2,1,0:T(8,128)S(1)} %reduce_sum.127, bf16[4,32,128]{2,1,0:T(8,128)(2,1)S(1)} %copy-done.2, f32[4,32]{1,0:T(4,128)S(1)} %add_rsqrt_fusion), kind=kOutput, calls=%fused_computation.48 | output fusion | flops 131327 | bytes 164352 | tf_op jit(solution)/shard_map/mul | solution.py:102
  (78 shorter events, 3.5 us)
Async XLA Ops:
  0.6 0.8 copy-start
  1.5 1.7 %copy-start.4 = (s32[16,12]{1,0:T(8,128)S(1)}, s32[16,12]{1,0:T(8,128)}, u32[]{:S(2)}) copy-start(s32[16,12]{1,0:T(8,128)} %param.15) | copy-start | bytes 2308
  3.0 1.0 copy-start.1
  4.0 1.5 %copy-start.2 = (bf16[4,32,128]{2,1,0:T(8,128)(2,1)S(1)}, bf16[4,32,128]{2,1,0:T(8,128)(2,1)}, u32[]{:S(2)}) copy-start(bf16[4,32,128]{2,1,0:T(8,128)(2,1)} %param.12) | copy-start | bytes 98308
  4.0 8.7 %copy-start.3 = (bf16[1,184,128]{2,1,0:T(8,128)(2,1)S(1)}, bf16[1,184,128]{2,1,0:T(8,128)(2,1)}, u32[]{:S(2)}) copy-start(bf16[1,184,128]{2,1,0:T(8,128)(2,1)} %param.13) | copy-start | bytes 141316
  44.8 16.7 %copy-start.6 = (u32[32]{0:T(128)S(1)}, u32[32]{0:T(128)}, u32[]{:S(2)}) copy-start(u32[32]{0:T(128)} %constant.111) | copy-start | bytes 388
  44.8 18.1 %copy-start.5 = (f32[4,12]{1,0:T(4,128)S(1)}, f32[4,12]{1,0:T(4,128)}, u32[]{:S(2)}) copy-start(f32[4,12]{1,0:T(4,128)} %param.17) | copy-start | bytes 580
where the time goes:
time: 103 us; the launch traced here: 102 us
  blocking collectives  59.1 us (57%)
  matrix products  21 us (20%)
  local copies, waits for them, and re-layouts  13.2 us (13%)
  other arithmetic  4.46 us (4%)
  loops' own time  2.94 us (3%)
  between operations  1.51 us (1%)
    all_gather x1, blocking collectives, local(): cached = lax.all_gather(shard_unit, 'batch', axis=0, tiled=True)  31.8 us
    dot_general x4, matrix products, token_terms(): jnp.einsum('bid,bktd->bkit', query_block, passages, preferred_element_typ...  12.1 us
    all_to_all x1, blocking collectives, local(): lax.all_to_all(partials, 'owner', split_axis=0, concat_axis=0, tiled=True)  9.38 us
    all_gather x1, blocking collectives, local(): gathered = lax.all_gather(sent_query, 'owner', axis=0, tiled=True)  6.99 us
    dot_general x2, matrix products, one_block(): jnp.einsum('bkit,bktd->bkid', weights, passages, preferred_element_type=j...  6.09 us
    unnamed x1, blocking collectives  5.77 us
    all_gather x1, blocking collectives, local(): grad_rows = lax.all_gather(grad_own, 'owner', axis=0, tiled=True)  5.18 us
    gather x4, local copies, waits for them, and re-layouts, block_inputs(): return (query_block, jnp.take(cached, pick_block, axis=0), length_block)  4.05 us

commit v1 on v0

--- a/solution.py
+++ b/solution.py
@@ -9,6 +9,27 @@
 STUDENT_GAIN = 2.0
 LOSS_SCALE = 64.0
 EPSILON = 1e-06
+
+
+def laid_out(blocks, dim):
+    shape = list(blocks.shape[1:])
+    shape[dim] *= blocks.shape[0]
+    return jnp.moveaxis(blocks, 0, dim).reshape(shape)
+
+
+def collected_by_bits(x, axis):
+    size, place = (lax.axis_size(axis), lax.axis_index(axis))
+    blocks, bit = (x[None], 1)
+    while bit < size:
+        other = lax.ppermute(blocks, axis, [(i, i ^ bit) for i in range(size)])
+        low = place & bit == 0
+        blocks = jnp.concatenate([jnp.where(low, blocks, other), jnp.where(low, other, blocks)])
+        bit *= 2
+    return blocks
+
+
+def doubled_up(value, axis, dim):
+    return laid_out(collected_by_bits(value, axis), dim)
 
 
 def unit_rows(values):
@@ -47,7 +68,7 @@
     sent_query = unit_query.astype(jnp.bfloat16)
     gathered = lax.all_gather(sent_query, "owner", axis=0, tiled=True)
     shard_unit = unit_rows(pool)[0].astype(jnp.bfloat16)
-    cached = lax.all_gather(shard_unit, "batch", axis=0, tiled=True)
+    cached = doubled_up(shard_unit, "batch", 0)
     group_rows = cached.shape[0]
     slot_ids = jnp.take(owner_map, candidates, axis=0)
     local_slot = slot_ids - my_group * group_rows

time: 103 us -> 82.3 us (0.80)
  blocking collectives: 59.1 us -> 26.3 us
  starting transfers between devices: 0 us -> 7.33 us
  waiting for transfers between devices: 0 us -> 2.92 us
  other arithmetic: 4.46 us -> 6.25 us
    all_gather x1 -> x0, blocking collectives: 31.8 us -> none  [local(): cached = lax.all_gather(shard_unit, 'batch', axis=0, tiled=True)]
    ppermute x0 -> x3, starting transfers between devices: none -> 7.33 us  [collected_by_bits(): other = lax.ppermute(blocks, axis, [(i, i ^ bit) for i in range(size)])]
    ppermute x0 -> x3, waiting for transfers between devices: none -> 2.92 us  [collected_by_bits(): other = lax.ppermute(blocks, axis, [(i, i ^ bit) for i in range(size)])]
    all_gather x1, blocking collectives: 6.99 us -> 5.87 us  [local(): gathered = lax.all_gather(sent_query, 'owner', axis=0, tiled=True)]
  transfers between devices with their start and end apart: 0 -> 3, of which waited for: 0 -> 2; matrix products, arithmetic and copies ran while one was open for 0% -> 7% of each run, Pallas kernels for 0% -> 0%
where the time goes in v1:
time: 82.3 us; the launch traced here: 81.6 us
  blocking collectives  26.3 us (32%)
  matrix products  21 us (26%)
  local copies, waits for them, and re-layouts  13.3 us (16%)
  starting transfers between devices  7.33 us (9%)
  other arithmetic  6.25 us (8%)
  loops' own time  2.94 us (4%)
  waiting for transfers between devices  2.92 us (4%)
  between operations  1.61 us (2%)
    dot_general x4, matrix products, token_terms(): jnp.einsum('bid,bktd->bkit', query_block, passages, preferred_element_typ...  12.1 us
    all_to_all x1, blocking collectives, local(): lax.all_to_all(partials, 'owner', split_axis=0, concat_axis=0, tiled=True)  9.38 us
    ppermute x3, starting transfers between devices, collected_by_bits(): other = lax.ppermute(blocks, axis, [(i, i ^ bit) for i in range(size)])  7.33 us
    dot_general x2, matrix products, one_block(): jnp.einsum('bkit,bktd->bkid', weights, passages, preferred_element_type=j...  6.09 us
    unnamed x1, blocking collectives  5.89 us
    all_gather x1, blocking collectives, local(): gathered = lax.all_gather(sent_query, 'owner', axis=0, tiled=True)  5.87 us
    all_gather x1, blocking collectives, local(): grad_rows = lax.all_gather(grad_own, 'owner', axis=0, tiled=True)  5.18 us
    gather x4, local copies, waits for them, and re-layouts, block_inputs(): return (query_block, jnp.take(cached, pick_block, axis=0), length_block)  4.05 us
  transfers between devices with their start and end apart: 3, of which 2 were waited for; matrix products, arithmetic and copies ran while one was open for 7% of the time, Pallas kernels for 0%

profile of v1, /device:TPU:0, one launch (start us, length us, event | category | flops | bytes accessed | tf_op | source)
XLA Modules:
  0.0 81.6 jit_solution(7939013639975664999)
XLA Ops:
  0.6 0.9 %fusion.29 = f32[184]{0:T(256)S(1)} fusion(bf16[1,184,128]{2,1,0:T(8,128)(2,1)} %param.13), kind=kLoop, calls=%fused_computation.55 | loop fusion | flops 70472 | bytes 47840 | tf_op jit(solution)/shard_map/reduce_sum | solution.py:37
  1.6 0.9 %fusion.38 = bf16[1,1,184,128]{3,2,0,1:T(8,128)(2,1)S(1)} fusion(bf16[1,184,128]{2,1,0:T(8,128)(2,1)} %param.13, f32[184]{0:T(256)S(1)} %add_rsqrt_fusion.1), kind=kLoop, calls=%fused_computation.72 | loop fusion | flops 70656 | bytes 94944 | tf_op jit(solution)/shard_map/broadcast_in_dim | solution.py:22
  2.5 3.0 %collective-permute-start = (bf16[1,1,184,128]{3,2,0,1:T(8,128)(2,1)S(1)}, bf16[1,1,184,128]{3,2,0,1:T(8,128)(2,1)S(1)}, u32[]{:S(2)}, u32[]{:S(2)}) collective-permute-start(bf16[1,1,184,128]{3,2,0,1:T(8,128)(2,1)S(1)} %fusion.38), channel_id=1, source_target_pairs={{0,4},{4,0},{8,12},{12,8},{16,20},{20,16},{24,28},{28,24},{1,5},{5... | collective-permute-start | bytes 141320 | tf_op jit(solution)/shard_map/ppermute | solution.py:24
  5.5 0.7 compare_select_fusion.2
  6.3 1.6 %gather_fusion.2 = s32[192]{0:T(256)S(1)} fusion(s32[32]{0:T(128)S(1)} %copy-done, s32[1024]{0:T(1024)S(1)} %pad_clamp_fusion.3), kind=kCustom, calls=%fused_computation.2 | custom fusion | bytes 2304 | tf_op jit(solution)/shard_map/jit(_take)/gather | solution.py:73
  8.8 1.2 %gather_fusion.3 = s32[96]{0:T(128)S(1)} fusion(s32[8]{0:T(128)S(1)} %copy-done.1, s32[1024]{0:T(1024)S(1)} %pad_clamp_fusion.2), kind=kCustom, calls=%fused_computation.3 | custom fusion | bytes 1152 | tf_op jit(solution)/shard_map/jit(_take)/gather | solution.py:81
  10.6 1.6 %collective-permute-start.1 = (bf16[2,1,184,128]{3,2,0,1:T(8,128)(2,1)S(1)}, bf16[2,1,184,128]{3,2,0,1:T(8,128)(2,1)S(1)}, u32[]{:S(2)}, u32[]{:S(2)}) collective-permute-start(bf16[2,1,184,128]{3,2,0,1:T(8,128)(2,1)S(1)} %pad_maximum_fusion.1), channel_id=1, source_target_pairs={{0,8},{4,12},{8,0},{12,4},{16,24},{20,28},{24,16},{28,20},{1,9},{5... | collective-permute-start | bytes 282632 | tf_op jit(solution)/shard_map/ppermute | solution.py:24
  13.8 1.5 %collective-permute-done.1 = bf16[2,1,184,128]{3,2,0,1:T(8,128)(2,1)S(1)} collective-permute-done((bf16[2,1,184,128]{3,2,0,1:T(8,128)(2,1)S(1)}, bf16[2,1,184,128]{3,2,0,1:T(8,128)(2,1)S(1)}, u32[]{:S(2)}, u32[]{:S(2)}) %collective-permute-start.1) | collective-permute-done | bytes 94240 | tf_op jit(solution)/shard_map/ppermute | solution.py:24
  15.3 2.7 %collective-permute-start.2 = (bf16[4,1,184,128]{3,2,0,1:T(8,128)(2,1)S(1)}, bf16[4,1,184,128]{3,2,0,1:T(8,128)(2,1)S(1)}, u32[]{:S(2)}, u32[]{:S(2)}) collective-permute-start(bf16[4,1,184,128]{3,2,0,1:T(8,128)(2,1)S(1)} %pad_maximum_fusion), channel_id=1, source_target_pairs={{0,16},{4,20},{8,24},{12,28},{16,0},{20,4},{24,8},{28,12},{1,17},{... | collective-permute-start | bytes 565256 | tf_op jit(solution)/shard_map/ppermute | solution.py:24
  18.1 5.9 %all_gather.6 = bf16[16,32,128]{2,1,0:T(8,128)(2,1)} all-gather(bf16[4,32,128]{2,1,0:T(8,128)(2,1)S(1)} %fusion.32), channel_id=1, replica_groups=mesh['batch'=8,'owner'=4] {'owner'}, dimensions={0}, use_global_device_ids=true | all-gather | bytes 163840 | tf_op jit(solution)/shard_map/all_gather | solution.py:69
  23.9 1.4 %collective-permute-done.2 = bf16[4,1,184,128]{3,2,0,1:T(8,128)(2,1)S(1)} collective-permute-done((bf16[4,1,184,128]{3,2,0,1:T(8,128)(2,1)S(1)}, bf16[4,1,184,128]{3,2,0,1:T(8,128)(2,1)S(1)}, u32[]{:S(2)}, u32[]{:S(2)}) %collective-permute-start.2) | collective-permute-done | bytes 188448 | tf_op jit(solution)/shard_map/ppermute | solution.py:24
  25.5 10.7 %while.20 = (s32[]{:T(128)}, f32[2,8,6]{2,1,0:T(8,128)S(1)}, s32[2]{0:T(128)S(1)}, s32[16,6]{1,0:T(8,128)S(1)}, s32[16,6]{1,0:T(8,128)S(1)}, /*index=5*/bf16[8,1...) while((s32[]{:T(128)}, f32[2,8,6]{2,1,0:T(8,128)S(1)}, ...), condition=%wide.region_8.10_spmd, body=%wide.region_5.9_spmd.sunk | while | flops 74615640 | bytes 6876823 | solution.py:97
  25.5 0.7 dynamic_slice.51
  26.9 1.0 %gather_fusion = bf16[48,184,128]{2,1,0:T(8,128)(2,1)S(1)} fusion(bf16[8,184,128]{2,1,0:T(8,128)(2,1)S(1)} %get-tuple-element.337, s32[1024]{0:T(1024)S(1)} %pad_clamp_fusion.6), kind=kCustom, calls=%fused_computation.clone.clone.1 | custom fusion | bytes 4522176 | tf_op jit(solution)/shard_map/while/body/eval_jaxpr/jit(_take)/gather | solution.py:87
  28.0 2.5 %fusion.57 = f32[8,6,32]{2,1,0:T(8,128)S(1)} fusion(bf16[8,6,184,128]{3,2,1,0:T(8,128)(2,1)S(1)} %bitcast.71, pred[8,6]{1,0:T(8,128)(4,1)S(1)} %get-tuple-element.297, s32[8,6]{1,0:T(8,128)S(1)} %get-tuple-element.298, bf16[16,32,128]{2,1,0:T(8,128)(2,1)} %get-tuple-element.338, s32[]{:T(128)S(6)} %select_n.186), kind=kOutput, calls=%fused_computation.8.clone.1 | convolution fusion | flops 74611200 | bytes 2332916 | tf_op jit(solution)/shard_map/while/body/eval_jaxpr/bid,bktd->bkit/dot_general | solution.py:42
  30.8 0.7 dynamic_slice.51
  32.3 1.0 %gather_fusion = bf16[48,184,128]{2,1,0:T(8,128)(2,1)S(1)} fusion(bf16[8,184,128]{2,1,0:T(8,128)(2,1)S(1)} %get-tuple-element.337, s32[1024]{0:T(1024)S(1)} %pad_clamp_fusion.6), kind=kCustom, calls=%fused_computation.clone.clone.1 | custom fusion | bytes 4522176 | tf_op jit(solution)/shard_map/while/body/eval_jaxpr/jit(_take)/gather | solution.py:87
  33.3 2.5 %fusion.57 = f32[8,6,32]{2,1,0:T(8,128)S(1)} fusion(bf16[8,6,184,128]{3,2,1,0:T(8,128)(2,1)S(1)} %bitcast.71, pred[8,6]{1,0:T(8,128)(4,1)S(1)} %get-tuple-element.297, s32[8,6]{1,0:T(8,128)S(1)} %get-tuple-element.298, bf16[16,32,128]{2,1,0:T(8,128)(2,1)} %get-tuple-element.338, s32[]{:T(128)S(6)} %select_n.186), kind=kOutput, calls=%fused_computation.8.clone.1 | convolution fusion | flops 74611200 | bytes 2332916 | tf_op jit(solution)/shard_map/while/body/eval_jaxpr/bid,bktd->bkit/dot_general | solution.py:42
  36.4 5.9 %all-reduce = f32[16,12]{1,0:T(8,128)S(1)} all-reduce(f32[16,12]{1,0:T(8,128)S(1)} %select_reduce_fusion.1), channel_id=2, replica_groups=mesh['batch'=8,'owner'=4] {'owner'}, use_global_device_ids=true, to_apply=%region_10.12.clone | all-reduce | flops 192 | bytes 1536
  42.4 0.7 multiply_reduce_fusion
  43.1 5.2 %all-gather = f32[4,4,12]{2,1,0:T(4,128)S(1)} all-gather(f32[1,4,12]{2,1,0:T(4,128)S(1)} %get-tuple-element.205), channel_id=1, replica_groups=mesh['batch'=8,'owner'=4] {'owner'}, dimensions={0}, use_global_device_ids=true | all-gather | bytes 960 | tf_op jit(solution)/shard_map/all_gather | solution.py:101
  48.4 22.7 %while.21 = (s32[]{:T(128)}, f32[2,8,32,128]{3,2,1,0:T(8,128)}, s32[2]{0:T(128)S(1)}, f32[16,6]{0,1:T(8,128)S(1)}, s32[16,6]{1,0:T(8,128)S(1)}, /*index=5*/s32[1...) while((s32[]{:T(128)}, f32[2,8,32,128]{3,2,1,0:T(8,128)}, ...), condition=%wide.region_16.18_spmd, body=%wide.region_14.17_spmd.sunk | while | flops 150739936 | bytes 13344207 | solution.py:116
  49.9 1.0 %gather_fusion.1 = bf16[48,184,128]{2,1,0:T(8,128)(2,1)S(1)} fusion(bf16[8,184,128]{2,1,0:T(8,128)(2,1)S(1)} %get-tuple-element.373, s32[1024]{0:T(1024)S(1)} %pad_clamp_fusion.7), kind=kCustom, calls=%fused_computation.1.clone.clone.1 | custom fusion | bytes 4522176 | tf_op jit(solution)/shard_map/while/body/eval_jaxpr/jit(_take)/gather | solution.py:87
  50.9 3.5 %bitcast_select_fusion.3 = f32[8,6,32,184]{3,2,1,0:T(8,128)} fusion(bf16[8,6,184,128]{3,2,1,0:T(8,128)(2,1)S(1)} %bitcast.72, pred[8,6]{1,0:T(8,128)(4,1)S(1)} %get-tuple-element.309, s32[8,6]{1,0:T(8,128)S(1)} %constant_dynamic-slice_fusion.4, bf16[16,32,128]{2,1,0:T(8,128)(2,1)} %get-tuple-element.374, s32[]{:T(128)S(6)} %select_n.190), kind=kOutput, calls=%fused_computation.25.clone.1 | convolution fusion | flops 74330112 | bytes 3457268 | tf_op jit(solution)/shard_map/while/body/eval_jaxpr/bid,bktd->bkit/dot_general | solution.py:42
  54.4 3.0 %fusion.62 = f32[8,6,32,128]{3,2,1,0:T(8,128)S(1)} fusion(bf16[8,6,184,128]{3,2,1,0:T(8,128)(2,1)S(1)} %bitcast.73, pred[8,6]{1,0:T(8,128)(4,1)S(1)} %get-tuple-element.309, f32[8,6,32,184]{3,2,1,0:T(8,128)} %bitcast_select_fusion.3), kind=kOutput, calls=%fused_computation.23.clone.1 | convolution fusion | flops 74049208 | bytes 4177968 | tf_op jit(solution)/shard_map/while/body/eval_jaxpr/bkit,bktd->bkid/dot_general | solution.py:112
  57.7 1.4 %fusion.63 = f32[8,1,32,128]{3,1,2,0:T(1,128)S(1)} fusion(f32[8,6,1,1]{1,2,3,0:T(1,128)S(1)} %copy.66, f32[8,6,32,128]{3,2,1,0:T(8,128)S(1)} %fusion.62), kind=kOutput, calls=%fused_computation.30.clone.1 | convolution fusion | flops 2359296 | bytes 917696 | tf_op jit(solution)/shard_map/while/body/eval_jaxpr/bk,bkid->bid/dot_general | solution.py:113
  61.2 1.0 %gather_fusion.1 = bf16[48,184,128]{2,1,0:T(8,128)(2,1)S(1)} fusion(bf16[8,184,128]{2,1,0:T(8,128)(2,1)S(1)} %get-tuple-element.373, s32[1024]{0:T(1024)S(1)} %pad_clamp_fusion.7), kind=kCustom, calls=%fused_computation.1.clone.clone.1 | custom fusion | bytes 4522176 | tf_op jit(solution)/shard_map/while/body/eval_jaxpr/jit(_take)/gather | solution.py:87
  62.2 3.5 %bitcast_select_fusion.3 = f32[8,6,32,184]{3,2,1,0:T(8,128)} fusion(bf16[8,6,184,128]{3,2,1,0:T(8,128)(2,1)S(1)} %bitcast.72, pred[8,6]{1,0:T(8,128)(4,1)S(1)} %get-tuple-element.309, s32[8,6]{1,0:T(8,128)S(1)} %constant_dynamic-slice_fusion.4, bf16[16,32,128]{2,1,0:T(8,128)(2,1)} %get-tuple-element.374, s32[]{:T(128)S(6)} %select_n.190), kind=kOutput, calls=%fused_computation.25.clone.1 | convolution fusion | flops 74330112 | bytes 3457268 | tf_op jit(solution)/shard_map/while/body/eval_jaxpr/bid,bktd->bkit/dot_general | solution.py:42
  65.8 3.0 %fusion.62 = f32[8,6,32,128]{3,2,1,0:T(8,128)S(1)} fusion(bf16[8,6,184,128]{3,2,1,0:T(8,128)(2,1)S(1)} %bitcast.73, pred[8,6]{1,0:T(8,128)(4,1)S(1)} %get-tuple-element.309, f32[8,6,32,184]{3,2,1,0:T(8,128)} %bitcast_select_fusion.3), kind=kOutput, calls=%fused_computation.23.clone.1 | convolution fusion | flops 74049208 | bytes 4177968 | tf_op jit(solution)/shard_map/while/body/eval_jaxpr/bkit,bktd->bkid/dot_general | solution.py:112
  69.0 1.4 %fusion.63 = f32[8,1,32,128]{3,1,2,0:T(1,128)S(1)} fusion(f32[8,6,1,1]{1,2,3,0:T(1,128)S(1)} %copy.66, f32[8,6,32,128]{3,2,1,0:T(8,128)S(1)} %fusion.62), kind=kOutput, calls=%fused_computation.30.clone.1 | convolution fusion | flops 2359296 | bytes 917696 | tf_op jit(solution)/shard_map/while/body/eval_jaxpr/bk,bkid->bid/dot_general | solution.py:113
  71.1 9.4 %all_to_all.5 = f32[4,4,32,128]{3,2,1,0:T(8,128)S(1)} all-to-all(f32[4,4,32,128]{3,2,1,0:T(8,128)} %bitcast.75), channel_id=1, replica_groups=mesh['batch'=8,'owner'=4] {'owner'}, dimensions={0} | all-to-all | bytes 524288 | tf_op jit(solution)/shard_map/all_to_all | solution.py:120
  80.5 1.1 %fusion.28 = f32[4,32,128]{2,1,0:T(8,128)} fusion(f32[4,32,128]{2,1,0:T(8,128)S(1)} %reduce_sum.127, bf16[4,32,128]{2,1,0:T(8,128)(2,1)S(1)} %copy-done.3, f32[4,32]{1,0:T(4,128)S(1)} %add_rsqrt_fusion), kind=kOutput, calls=%fused_computation.48 | output fusion | flops 131327 | bytes 164352 | tf_op jit(solution)/shard_map/mul | solution.py:123
  (89 shorter events, 7.0 us)
Async XLA Ops:
  0.6 5.7 %copy-start = (s32[32]{0:T(128)S(1)}, s32[32]{0:T(128)}, u32[]{:S(2)}) copy-start(s32[32]{0:T(128)} %param.16) | copy-start | bytes 388
  2.5 8.1 %collective-permute-start = (bf16[1,1,184,128]{3,2,0,1:T(8,128)(2,1)S(1)}, bf16[1,1,184,128]{3,2,0,1:T(8,128)(2,1)S(1)}, u32[]{:S(2)}, u32[]{:S(2)}) collective-permute-start(bf16[1,1,184,128]{3,2,0,1:T(8,128)(2,1)S(1)} %fusion.38), channel_id=1, source_target_pairs={{0,4},{4,0},{8,12},{12,8},{16,20},{20,16},{24,28},{28,24},{1,5},{5... | collective-permute-start | bytes 141320 | tf_op jit(solution)/shard_map/ppermute | solution.py:24
  6.3 1.7 %copy-start.4 = (s32[16,12]{1,0:T(8,128)S(1)}, s32[16,12]{1,0:T(8,128)}, u32[]{:S(2)}) copy-start(s32[16,12]{1,0:T(8,128)} %param.15) | copy-start | bytes 2308
  7.9 0.9 %copy-start.1 = (s32[8]{0:T(128)S(1)}, s32[8]{0:T(128)}, u32[]{:S(2)}) copy-start(s32[8]{0:T(128)} %param.14) | copy-start | bytes 100
  8.8 1.4 %copy-start.3 = (bf16[4,32,128]{2,1,0:T(8,128)(2,1)S(1)}, bf16[4,32,128]{2,1,0:T(8,128)(2,1)}, u32[]{:S(2)}) copy-start(bf16[4,32,128]{2,1,0:T(8,128)(2,1)} %param.12) | copy-start | bytes 98308
  8.8 1.7 %copy-start.2 = (bf16[1,184,128]{2,1,0:T(8,128)(2,1)S(1)}, bf16[1,184,128]{2,1,0:T(8,128)(2,1)}, u32[]{:S(2)}) copy-start(bf16[1,184,128]{2,1,0:T(8,128)(2,1)} %param.13) | copy-start | bytes 141316
  8.8 3.5 %copy-start.5 = (f32[4,12]{1,0:T(4,128)S(1)}, f32[4,12]{1,0:T(4,128)}, u32[]{:S(2)}) copy-start(f32[4,12]{1,0:T(4,128)} %param.17) | copy-start | bytes 580
  8.8 3.6 %copy-start.6 = (u32[32]{0:T(128)S(1)}, u32[32]{0:T(128)}, u32[]{:S(2)}) copy-start(u32[32]{0:T(128)} %constant.120) | copy-start | bytes 388
  10.6 4.6 %collective-permute-start.1 = (bf16[2,1,184,128]{3,2,0,1:T(8,128)(2,1)S(1)}, bf16[2,1,184,128]{3,2,0,1:T(8,128)(2,1)S(1)}, u32[]{:S(2)}, u32[]{:S(2)}) collective-permute-start(bf16[2,1,184,128]{3,2,0,1:T(8,128)(2,1)S(1)} %pad_maximum_fusion.1), channel_id=1, source_target_pairs={{0,8},{4,12},{8,0},{12,4},{16,24},{20,28},{24,16},{28,20},{1,9},{5... | collective-permute-start | bytes 282632 | tf_op jit(solution)/shard_map/ppermute | solution.py:24
  15.3 10.0 %collective-permute-start.2 = (bf16[4,1,184,128]{3,2,0,1:T(8,128)(2,1)S(1)}, bf16[4,1,184,128]{3,2,0,1:T(8,128)(2,1)S(1)}, u32[]{:S(2)}, u32[]{:S(2)}) collective-permute-start(bf16[4,1,184,128]{3,2,0,1:T(8,128)(2,1)S(1)} %pad_maximum_fusion), channel_id=1, source_target_pairs={{0,16},{4,20},{8,24},{12,28},{16,0},{20,4},{24,8},{28,12},{1,17},{... | collective-permute-start | bytes 565256 | tf_op jit(solution)/shard_map/ppermute | solution.py:24
